TPU v7x, 512 devices: a whole 4x4x16 slice. The times are simulated.
512 devices in a mesh: seq: 128 (over x_hi, z, y), head: 4 (over x_lo, core).
Axes of the slice: x: 4 (x_hi: 2, x_lo: 2; x = x_hi * 2 + x_lo), y: 4, z: 16, core: 2. Of those that a mesh axis runs over, the one named last changes fastest.
Arguments:
- layer_input: bfloat16 [16384, 2688], P('seq'), may hold values from -32 to 32
- grad_out: bfloat16 [16384, 2688], P('seq'), may hold values from -6 to 6
- doc_start: int32 [16384], P('seq'), may hold values from 0 to 16383, as said below
- w_query: bfloat16 [2688, 2048], P('seq', 'head'), may hold values from -0.125 to 0.125
- key_weight: bfloat16 [2688, 1024], P('seq', 'head'), may hold values from -0.125 to 0.125
- value_weight: bfloat16 [2688, 1024], P('seq', 'head'), may hold values from -0.125 to 0.125
- w_out: bfloat16 [2048, 2688], P('head', 'seq'), may hold values from -0.125 to 0.125
- q_gain: float32 [128], replicated, may hold values from 0.5 to 5, as said below
- key_norm_gain: float32 [128], replicated, may hold values from 0.5 to 5, as said below
Outputs:
- fisher_value: float32 [2688, 1024], P('seq', 'head')
- grad_input: bfloat16 [16384, 2688], P(('seq', 'head'))
Inputs may be any that keep to these rules, and one draw needn't show every extreme that they name: doc_start[t] is the first token of the document holding token t: it never falls, doc_start[t] <= t, doc_start[0] = 0, and the last token begins a document of its own. `q_gain`: positive. `key_norm_gain`: positive.
All inputs are finite; a program needn't handle non-finite values.
Results may differ from a plain program's by a relative error of at most 0.011.
Values may be sent and summed in bfloat16 or wider, within the bound.
A program may use at most 64 MiB of HBM per device.

v0:
```python
import math
import jax
import jax.numpy as jnp
from jax import lax
from jax.sharding import PartitionSpec as P

HEAD_SIZE = 128
QSCALE = 168
WINDOW = 1024
REACH = 8


def passed_along(array, axis, by):
    peers = lax.axis_size(axis)
    pairs = [(i, i + by) for i in range(peers) if 0 <= i + by < peers]
    return lax.ppermute(array, axis, pairs)


def rotary_normed(unrotated_rows, gain_vec, token_positions, head_count):
    tokens_here = unrotated_rows.shape[0]
    entries = unrotated_rows.reshape(tokens_here, head_count, HEAD_SIZE)
    mean_sq = jnp.mean(entries * entries, axis=-1, keepdims=True)
    normed = entries * lax.rsqrt(mean_sq + 1e-06) * gain_vec
    half_dim = HEAD_SIZE // 2
    frequency = jnp.exp(jnp.arange(half_dim).astype(jnp.float32) * (-math.log(10000.0) / half_dim))
    angles = token_positions.astype(jnp.float32)[:, None] * frequency[None, :]
    cosine = jnp.cos(angles)[:, None, :]
    sine_part = jnp.sin(angles)[:, None, :]
    first_half = normed[..., :half_dim]
    second_half = normed[..., half_dim:]
    return jnp.concatenate(
        [
            first_half * cosine - second_half * sine_part,
            second_half * cosine + first_half * sine_part,
        ],
        axis=-1,
    )


def attend(query_blk, key_blk, value_blk, dattn_blk, visible):
    scale = float(QSCALE) ** (-0.5)
    scores = (
        jnp.einsum("qhgd,chd->hgqc", query_blk, key_blk, preferred_element_type=jnp.float32) * scale
    )
    scores = jnp.where(visible[None, None], scores, -jnp.inf)
    top_score = jnp.max(scores, axis=-1, keepdims=True)
    expd = jnp.exp(scores - top_score)
    probs = expd / jnp.sum(expd, axis=-1, keepdims=True)
    probs_b = probs.astype(jnp.bfloat16)
    dprobs = jnp.einsum("qhgd,chd->hgqc", dattn_blk, value_blk, preferred_element_type=jnp.float32)
    delta = jnp.sum(probs * dprobs, axis=-1, keepdims=True)
    dscores = (probs * (dprobs - delta)).astype(jnp.bfloat16)
    dquery = (
        jnp.einsum("hgqc,chd->qhgd", dscores, key_blk, preferred_element_type=jnp.float32) * scale
    )
    dkey = (
        jnp.einsum("hgqc,qhgd->chd", dscores, query_blk, preferred_element_type=jnp.float32) * scale
    )
    value_grad = jnp.einsum(
        "hgqc,qhgd->chd", probs_b, dattn_blk, preferred_element_type=jnp.float32
    )
    return (dquery, dkey, value_grad)


def on_device(
    layer_input,
    grad_out,
    doc_start,
    w_query,
    key_weight,
    value_weight,
    w_out,
    q_gain,
    key_norm_gain,
):
    tok_rows = layer_input.shape[0]
    full_query, full_key, full_value = (
        lax.all_gather(w_query, "seq", axis=0, tiled=True),
        lax.all_gather(key_weight, "seq", axis=0, tiled=True),
        lax.all_gather(value_weight, "seq", axis=0, tiled=True),
    )
    query_heads = full_query.shape[1] // HEAD_SIZE
    kv_heads = full_key.shape[1] // HEAD_SIZE
    group_width = query_heads // kv_heads
    seq_index = lax.axis_index("seq")
    token_index = seq_index * tok_rows + jnp.arange(tok_rows, dtype=jnp.int32)
    token_positions = token_index - doc_start
    query_raw = jnp.dot(layer_input, full_query, preferred_element_type=jnp.float32)
    key_unrotated = jnp.dot(layer_input, full_key, preferred_element_type=jnp.float32)
    value_row_matrix = jnp.dot(layer_input, full_value, preferred_element_type=jnp.float32).astype(
        jnp.bfloat16
    )
    query_full, query_back = jax.vjp(
        lambda unrotated_rows: rotary_normed(unrotated_rows, q_gain, token_positions, query_heads),
        query_raw,
    )
    key_complete, key_backward = jax.vjp(
        lambda unrotated_rows: rotary_normed(
            unrotated_rows, key_norm_gain, token_positions, kv_heads
        ),
        key_unrotated,
    )
    query_row_matrix = query_full.astype(jnp.bfloat16)
    key_row_matrix = key_complete.astype(jnp.bfloat16)
    attention_grad = lax.dot_general(
        grad_out,
        lax.all_gather(w_out, "seq", axis=1, tiled=True),
        (((1,), (1,)), ((), ())),
        preferred_element_type=jnp.float32,
    ).astype(jnp.bfloat16)
    key_value = jnp.stack(
        [key_row_matrix.reshape(tok_rows, kv_heads * HEAD_SIZE), value_row_matrix]
    )
    earlier = [key_value]
    for distance in range(1, REACH + 1):
        earlier.append(passed_along(key_value, "seq", distance))
    context = jnp.concatenate([earlier[distance] for distance in range(REACH, -1, -1)], axis=1)
    context_len = context.shape[1]
    key_index = (seq_index - REACH) * tok_rows + jnp.arange(context_len, dtype=jnp.int32)
    visible = (
        (key_index[None, :] >= doc_start[:, None])
        & (key_index[None, :] <= token_index[:, None])
        & (token_index[:, None] - key_index[None, :] < WINDOW)
    )
    dquery, dkey, value_grad = attend(
        query_row_matrix.reshape(tok_rows, kv_heads, group_width, HEAD_SIZE),
        context[0].reshape(context_len, kv_heads, HEAD_SIZE),
        context[1].reshape(context_len, kv_heads, HEAD_SIZE),
        attention_grad.reshape(tok_rows, kv_heads, group_width, HEAD_SIZE),
        visible,
    )
    key_grads = jnp.stack(
        [
            dkey.reshape(context_len, kv_heads * HEAD_SIZE),
            value_grad.reshape(context_len, kv_heads * HEAD_SIZE),
        ]
    )

    def block_of(distance):
        first_row = (REACH - distance) * tok_rows
        return key_grads[:, first_row : first_row + tok_rows]

    owned_grads = block_of(0)
    for distance in range(1, REACH + 1):
        owned_grads = owned_grads + passed_along(block_of(distance), "seq", -distance)
    key_total = owned_grads[0].reshape(tok_rows, kv_heads, HEAD_SIZE)
    value_total = owned_grads[1]
    dquery_raw = query_back(dquery.reshape(tok_rows, query_heads, HEAD_SIZE))[0].astype(
        jnp.bfloat16
    )
    dkey_raw = key_backward(key_total)[0].astype(jnp.bfloat16)
    dvalue_rows = value_total.astype(jnp.bfloat16)
    squares = jnp.square(layer_input.astype(jnp.float32))
    value_sq = value_total * value_total
    all_tokens = lax.axis_size("seq") * tok_rows
    fisher_term = lax.dot_general(
        squares,
        value_sq,
        (((0,), (0,)), ((), ())),
        precision=lax.Precision.HIGHEST,
        preferred_element_type=jnp.float32,
    )
    fisher_value = (
        lax.psum_scatter(fisher_term, "seq", scatter_dimension=0, tiled=True) / all_tokens
    )
    contract = (((1,), (1,)), ((), ()))
    total = lax.dot_general(dquery_raw, full_query, contract, preferred_element_type=jnp.float32)
    total = total + lax.dot_general(
        dkey_raw, full_key, contract, preferred_element_type=jnp.float32
    )
    grad_input = lax.psum_scatter(
        total
        + lax.dot_general(dvalue_rows, full_value, contract, preferred_element_type=jnp.float32),
        "head",
        scatter_dimension=0,
        tiled=True,
    ).astype(jnp.bfloat16)
    return (fisher_value, grad_input)


def solution(mesh):
    in_specs = (
        P("seq", None),
        P("seq", None),
        P("seq"),
        P("seq", "head"),
        P("seq", "head"),
        P("seq", "head"),
        P("head", "seq"),
        P(),
        P(),
    )
    out_specs = (P("seq", "head"), P(("seq", "head"), None))
    return jax.shard_map(
        on_device, mesh=mesh, in_specs=in_specs, out_specs=out_specs, check_vma=False
    )
```

profile of v0, /device:TPU:32, one launch (start us, length us, event | category | flops | bytes accessed | tf_op | source)
XLA Modules:
  0.0 1421.1 jit_solution(520456489507171597)
XLA Ops:
  11.1 204.0 %all-gather.11.cloned.1.call-done = bf16[128,21,256]{2,1,0:T(8,128)(2,1)} async-done(((bf16[1,21,256]{2,1,0:T(8,128)(2,1)}), bf16[128,21,256]{2,1,0:T(8,128)(2,1)}) %all-gather.11.cloned.1.call-update) | async-done | bytes 1376272 | tf_op jit(solution)/shard_map/all_gather | solution.py:79
  215.1 2.4 reshape.224
  219.4 192.9 %all-gather.13.cloned.1.call-done = bf16[128,21,256]{2,1,0:T(8,128)(2,1)} async-done(((bf16[1,21,256]{2,1,0:T(8,128)(2,1)}), bf16[128,21,256]{2,1,0:T(8,128)(2,1)}) %all-gather.13.cloned.1.call-update) | async-done | bytes 1376272 | tf_op jit(solution)/shard_map/all_gather | solution.py:80
  412.2 2.4 reshape.226
  415.1 5.5 collective-permute-start.1
  420.6 3.4 collective-permute-start
  424.9 2.5 collective-permute-start.7
  427.4 4.8 collective-permute-start.6
  432.2 2.8 collective-permute-start.5
  435.0 5.1 collective-permute-start.2
  440.2 3.0 collective-permute-start.3
  443.2 5.7 collective-permute-start.4
  448.9 2.5 collective-permute-done.4
  452.7 1.8 copy.100
  454.5 177.1 %all-gather.15.cloned.1.call-done = bf16[128,21,512]{2,1,0:T(8,128)(2,1)} async-done(((bf16[1,21,512]{2,1,0:T(8,128)(2,1)}), bf16[128,21,512]{2,1,0:T(8,128)(2,1)}) %all-gather.15.cloned.1.call-update) | async-done | bytes 2752528 | tf_op jit(solution)/shard_map/all_gather | solution.py:107
  631.6 3.9 reshape.228
  638.3 211.3 %all-gather.9.cloned.1.call-done = bf16[128,21,512]{2,1,0:T(8,128)(2,1)} async-done(((bf16[1,21,512]{2,1,0:T(8,128)(2,1)}), bf16[128,21,512]{2,1,0:T(8,128)(2,1)}) %all-gather.9.cloned.1.call-update) | async-done | bytes 2752528 | tf_op jit(solution)/shard_map/all_gather | solution.py:78
  849.6 3.9 reshape.222
  853.5 2.4 fusion.52
  857.6 1.8 multiply_reduce_fusion.2
  864.7 3.5 fusion.51
  868.2 3.6 fusion.10
  871.8 2.5 multiply_reduce_fusion
  880.6 1.7 copy.110
  884.3 1.9 multiply_reduce_fusion.1
  887.1 3.0 fusion.26
  890.1 4.6 collective-permute-start.8
  894.7 2.9 collective-permute-start.9
  897.6 1.9 collective-permute-start.10
  900.3 1.9 collective-permute-start.11
  906.7 3.7 collective-permute-done.9
  913.0 2.1 fusion.33
  915.1 28.1 %collective-permute-done.11 = f32[2,128,256]{1,2,0:T(8,128)S(1)} collective-permute-done((f32[2,128,256]{1,2,0:T(8,128)}, f32[2,128,256]{1,2,0:T(8,128)S(1)}, u32[]{:S(2)}, u32[]{:S(2)}) %collective-permute-start.11) | collective-permute-done | bytes 262176 | tf_op jit(solution)/shard_map/ppermute | solution.py:16
  944.5 3.9 fusion.7
  960.8 369.8 %fusion = f32[24,256]{1,0:T(8,128)S(1)} fusion(f32[2688,256]{1,0:T(8,128)S(1)} %copy-done.7), kind=kCustom, calls=%all-reduce-scatter | all-reduce-scatter fusion | flops 786433 | bytes 2779136
  1334.5 22.1 %collective-permute-start.28 = (f32[24,256]{1,0:T(8,128)S(1)}, f32[24,256]{1,0:T(8,128)S(1)}, u32[]{:S(2)}, u32[]{:S(2)}) collective-permute-start(f32[24,256]{1,0:T(8,128)S(1)} %fusion), channel_id=1, source_target_pairs={{0,52},{4,56},{8,60},{12,64},{16,68},{20,72},{24,76},{28,80},{32,8... | collective-permute-start | bytes 73736
  1358.0 1.8 collective-permute-start.26
  1359.8 12.5 collective-permute-start.25
  1372.3 1.9 collective-permute-start.24
  1374.2 2.5 collective-permute-start.23
  1376.8 3.1 collective-permute-start.22
  1379.9 4.9 collective-permute-start.21
  1386.1 8.2 collective-permute-start.19
  1394.3 3.7 collective-permute-start.18
  1398.1 4.2 collective-permute-start.17
  1402.3 1.9 collective-permute-start.16
  1406.2 3.9 collective-permute-done.16
  1410.2 2.1 concatenate.21
  (168 shorter events, 58.4 us)
Async XLA Ops:
  7.2 628.3 %copy-start = (bf16[128,2688]{1,0:T(8,128)(2,1)S(1)}, bf16[128,2688]{1,0:T(8,128)(2,1)}, u32[]{:S(2)}) copy-start(bf16[128,2688]{1,0:T(8,128)(2,1)} %param.10) | copy-start | bytes 2064388
  7.2 207.9 %all-gather.11.cloned.1.call-start = ((), (), s32[]{:S(2)}) async-start(), calls=%async_computation.3 | async-start | bytes 1585152 | tf_op jit(solution)/shard_map/all_gather | solution.py:79
  7.9 404.3 %all-gather.13.cloned.1.call-start = ((), (), s32[]{:S(2)}) async-start(), calls=%async_computation.4 | async-start | bytes 1585152 | tf_op jit(solution)/shard_map/all_gather | solution.py:80
  8.7 622.9 %all-gather.15.cloned.1.call-start = ((), (), s32[]{:S(2)}) async-start(), calls=%async_computation.5 | async-start | bytes 3170304 | tf_op jit(solution)/shard_map/all_gather | solution.py:107
  9.4 840.3 %all-gather.9.cloned.1.call-start = ((), (), s32[]{:S(2)}) async-start(), calls=%async_computation.2 | async-start | bytes 3170304 | tf_op jit(solution)/shard_map/all_gather | solution.py:78
  10.0 1402.9 %reduce-scatter.4.cloned.1.call-start = ((), (), s32[]{:S(2)}) async-start(), calls=%async_computation.1 | async-start | bytes 1720320 | tf_op jit(solution)/shard_map/reduce_scatter | solution.py:171
  11.0 207.8 %copy-start.18 = (f32[128,64]{1,0:T(8,128)}, f32[128,64]{1,0:T(8,128)S(1)}, u32[]{:S(2)}) copy-start(f32[128,64]{1,0:T(8,128)S(1)} %get-tuple-element.25) | copy-start | bytes 98308
  11.0 206.4 %copy-start.5 = (bf16[128,2688]{1,0:T(8,128)(2,1)S(1)}, bf16[128,2688]{1,0:T(8,128)(2,1)}, u32[]{:S(2)}) copy-start(bf16[128,2688]{1,0:T(8,128)(2,1)} %param.9) | copy-start | bytes 2064388
  217.9 196.7 %copy-start.11 = (f32[128,2,128]{2,1,0:T(2,128)}, f32[128,2,128]{2,1,0:T(2,128)S(1)}, u32[]{:S(2)}) copy-start(f32[128,2,128]{2,1,0:T(2,128)S(1)} %reshape.218) | copy-start | bytes 393220
  218.6 196.0 %copy-start.21 = (f32[128,2]{1,0:T(8,128)}, f32[128,2]{1,0:T(8,128)S(1)}, u32[]{:S(2)}) copy-start(f32[128,2]{1,0:T(8,128)S(1)} %copy.76) | copy-start | bytes 3076
  414.7 25.5 %copy-start.3 = (bf16[2688,256]{1,0:T(8,128)(2,1)}, bf16[2688,256]{1,0:T(8,128)(2,1)S(1)}, u32[]{:S(2)}) copy-start(bf16[2688,256]{1,0:T(8,128)(2,1)S(1)} %reshape.226) | copy-start | bytes 4128772
  414.7 9.3 copy-start.26
  415.1 25.1 %collective-permute-start.1 = (bf16[2,128,256]{2,1,0:T(8,128)(2,1)S(1)}, bf16[2,128,256]{2,1,0:T(8,128)(2,1)S(1)}, u32[]{:S(2)}, u32[]{:S(2)}) collective-permute-start(bf16[2,128,256]{2,1,0:T(8,128)(2,1)S(1)} %pad_maximum_fusion.2), channel_id=1, source_target_pairs={{0,28},{4,32},{8,36},{12,40},{16,44},{20,48},{24,52},{28,56},{32,6... | collective-permute-start | bytes 393224 | tf_op jit(solution)/shard_map/ppermute | solution.py:16
  420.6 14.4 %collective-permute-start = (bf16[2,128,256]{2,1,0:T(8,128)(2,1)S(1)}, bf16[2,128,256]{2,1,0:T(8,128)(2,1)S(1)}, u32[]{:S(2)}, u32[]{:S(2)}) collective-permute-start(bf16[2,128,256]{2,1,0:T(8,128)(2,1)S(1)} %pad_maximum_fusion.2), channel_id=1, source_target_pairs={{0,32},{4,36},{8,40},{12,44},{16,48},{20,52},{24,56},{28,60},{32,6... | collective-permute-start | bytes 393224 | tf_op jit(solution)/shard_map/ppermute | solution.py:16
  424.9 26.6 %collective-permute-start.7 = (bf16[2,128,256]{2,1,0:T(8,128)(2,1)S(1)}, bf16[2,128,256]{2,1,0:T(8,128)(2,1)S(1)}, u32[]{:S(2)}, u32[]{:S(2)}) collective-permute-start(bf16[2,128,256]{2,1,0:T(8,128)(2,1)S(1)} %pad_maximum_fusion.2), channel_id=1, source_target_pairs={{0,4},{4,8},{8,12},{12,16},{16,20},{20,24},{24,28},{28,32},{32,36}... | collective-permute-start | bytes 393224 | tf_op jit(solution)/shard_map/ppermute | solution.py:16
  427.4 24.1 %collective-permute-start.6 = (bf16[2,128,256]{2,1,0:T(8,128)(2,1)S(1)}, bf16[2,128,256]{2,1,0:T(8,128)(2,1)S(1)}, u32[]{:S(2)}, u32[]{:S(2)}) collective-permute-start(bf16[2,128,256]{2,1,0:T(8,128)(2,1)S(1)} %pad_maximum_fusion.2), channel_id=1, source_target_pairs={{0,8},{4,12},{8,16},{12,20},{16,24},{20,28},{24,32},{28,36},{32,40... | collective-permute-start | bytes 393224 | tf_op jit(solution)/shard_map/ppermute | solution.py:16
  432.2 19.2 %collective-permute-start.5 = (bf16[2,128,256]{2,1,0:T(8,128)(2,1)S(1)}, bf16[2,128,256]{2,1,0:T(8,128)(2,1)S(1)}, u32[]{:S(2)}, u32[]{:S(2)}) collective-permute-start(bf16[2,128,256]{2,1,0:T(8,128)(2,1)S(1)} %pad_maximum_fusion.2), channel_id=1, source_target_pairs={{0,12},{4,16},{8,20},{12,24},{16,28},{20,32},{24,36},{28,40},{32,4... | collective-permute-start | bytes 393224 | tf_op jit(solution)/shard_map/ppermute | solution.py:16
  435.0 8.1 collective-permute-start.2
  440.2 8.8 collective-permute-start.3
  443.2 8.2 collective-permute-start.4
  890.1 15.2 %collective-permute-start.8 = (f32[2,128,256]{1,2,0:T(8,128)}, f32[2,128,256]{1,2,0:T(8,128)}, u32[]{:S(2)}, u32[]{:S(2)}) collective-permute-start(f32[2,128,256]{1,2,0:T(8,128)} %get-tuple-element.2), channel_id=1, source_target_pairs={{4,0},{8,4},{12,8},{16,12},{20,16},{24,20},{28,24},{32,28},{36,32}... | collective-permute-start | bytes 786440 | tf_op jit(solution)/shard_map/ppermute | solution.py:16
  894.7 15.6 %collective-permute-start.9 = (f32[2,128,256]{1,2,0:T(8,128)}, f32[2,128,256]{1,2,0:T(8,128)}, u32[]{:S(2)}, u32[]{:S(2)}) collective-permute-start(f32[2,128,256]{1,2,0:T(8,128)} %get-tuple-element.3), channel_id=1, source_target_pairs={{8,0},{12,4},{16,8},{20,12},{24,16},{28,20},{32,24},{36,28},{40,32... | collective-permute-start | bytes 786440 | tf_op jit(solution)/shard_map/ppermute | solution.py:16
  897.6 14.0 collective-permute-start.10
  900.3 42.8 %collective-permute-start.11 = (f32[2,128,256]{1,2,0:T(8,128)}, f32[2,128,256]{1,2,0:T(8,128)S(1)}, u32[]{:S(2)}, u32[]{:S(2)}) collective-permute-start(f32[2,128,256]{1,2,0:T(8,128)} %get-tuple-element.5), channel_id=1, source_target_pairs={{16,0},{20,4},{24,8},{28,12},{32,16},{36,20},{40,24},{44,28},{48,3... | collective-permute-start | bytes 786440 | tf_op jit(solution)/shard_map/ppermute | solution.py:16
  902.2 40.9 %collective-permute-start.12 = (f32[2,128,256]{1,2,0:T(8,128)}, f32[2,128,256]{1,2,0:T(8,128)S(1)}, u32[]{:S(2)}, u32[]{:S(2)}) collective-permute-start(f32[2,128,256]{1,2,0:T(8,128)} %get-tuple-element.6), channel_id=1, source_target_pairs={{20,0},{24,4},{28,8},{32,12},{36,16},{40,20},{44,24},{48,28},{52,3... | collective-permute-start | bytes 786440 | tf_op jit(solution)/shard_map/ppermute | solution.py:16
  905.4 37.8 %collective-permute-start.13 = (f32[2,128,256]{1,2,0:T(8,128)}, f32[2,128,256]{1,2,0:T(8,128)S(1)}, u32[]{:S(2)}, u32[]{:S(2)}) collective-permute-start(f32[2,128,256]{1,2,0:T(8,128)} %get-tuple-element.7), channel_id=1, source_target_pairs={{24,0},{28,4},{32,8},{36,12},{40,16},{44,20},{48,24},{52,28},{56,3... | collective-permute-start | bytes 786440 | tf_op jit(solution)/shard_map/ppermute | solution.py:16
  910.3 32.8 %collective-permute-start.15 = (f32[2,128,256]{1,2,0:T(8,128)}, f32[2,128,256]{1,2,0:T(8,128)S(1)}, u32[]{:S(2)}, u32[]{:S(2)}) collective-permute-start(f32[2,128,256]{1,2,0:T(8,128)} %get-tuple-element.8), channel_id=1, source_target_pairs={{32,0},{36,4},{40,8},{44,12},{48,16},{52,20},{56,24},{60,28},{64,3... | collective-permute-start | bytes 786440 | tf_op jit(solution)/shard_map/ppermute | solution.py:16
  911.6 31.5 %collective-permute-start.14 = (f32[2,128,256]{1,2,0:T(8,128)}, f32[2,128,256]{1,2,0:T(8,128)S(1)}, u32[]{:S(2)}, u32[]{:S(2)}) collective-permute-start(f32[2,128,256]{1,2,0:T(8,128)} %get-tuple-element.9), channel_id=1, source_target_pairs={{28,0},{32,4},{36,8},{40,12},{44,16},{48,20},{52,24},{56,28},{60,3... | collective-permute-start | bytes 786440 | tf_op jit(solution)/shard_map/ppermute | solution.py:16
  912.9 30.2 %copy-start.8 = (f32[2,128,1152]{2,1,0:T(8,128)S(1)}, f32[2,128,1152]{2,1,0:T(8,128)}, u32[]{:S(2)}) copy-start(f32[2,128,1152]{2,1,0:T(8,128)} %fusion.6) | copy-start | bytes 3538948
  913.0 30.2 %copy-start.10 = (f32[2,128,1152,1]{2,1,3,0:T(8,128)S(1)}, f32[2,128,1152,1]{2,1,3,0:T(8,128)}, u32[]{:S(2)}) copy-start(f32[2,128,1152,1]{2,1,3,0:T(8,128)} %fusion.10) | copy-start | bytes 3538948
  915.1 29.4 %copy-start.6 = (bf16[128,2688]{1,0:T(8,128)(2,1)S(1)}, bf16[128,2688]{1,0:T(8,128)(2,1)}, u32[]{:S(2)}) copy-start(bf16[128,2688]{1,0:T(8,128)(2,1)} %param.9) | copy-start | bytes 2064388
  944.5 12.6 copy-start.9
  1330.6 27.3 %collective-permute-start.31 = (f32[21,256]{1,0:T(8,128)S(1)}, f32[21,256]{1,0:T(8,128)S(1)}, u32[]{:S(2)}, u32[]{:S(2)}) collective-permute-start(f32[21,256]{1,0:T(8,128)S(1)} %slice.92), channel_id=1, source_target_pairs={{0,64},{4,68},{8,72},{12,76},{16,80},{20,84},{24,88},{28,92},{32,9... | collective-permute-start | bytes 64520
  1331.9 27.9 %collective-permute-start.30 = (f32[24,256]{1,0:T(8,128)S(1)}, f32[24,256]{1,0:T(8,128)S(1)}, u32[]{:S(2)}, u32[]{:S(2)}) collective-permute-start(f32[24,256]{1,0:T(8,128)S(1)} %fusion), channel_id=1, source_target_pairs={{0,60},{4,64},{8,68},{12,72},{16,76},{20,80},{24,84},{28,88},{32,9... | collective-permute-start | bytes 73736
  1333.2 39.1 %collective-permute-start.29 = (f32[24,256]{1,0:T(8,128)S(1)}, f32[24,256]{1,0:T(8,128)S(1)}, u32[]{:S(2)}, u32[]{:S(2)}) collective-permute-start(f32[24,256]{1,0:T(8,128)S(1)} %fusion), channel_id=1, source_target_pairs={{0,56},{4,60},{8,64},{12,68},{16,72},{20,76},{24,80},{28,84},{32,8... | collective-permute-start | bytes 73736
  1334.5 39.7 %collective-permute-start.28 = (f32[24,256]{1,0:T(8,128)S(1)}, f32[24,256]{1,0:T(8,128)S(1)}, u32[]{:S(2)}, u32[]{:S(2)}) collective-permute-start(f32[24,256]{1,0:T(8,128)S(1)} %fusion), channel_id=1, source_target_pairs={{0,52},{4,56},{8,60},{12,64},{16,68},{20,72},{24,76},{28,80},{32,8... | collective-permute-start | bytes 73736
  1356.6 20.1 %collective-permute-start.27 = (f32[24,256]{1,0:T(8,128)S(1)}, f32[24,256]{1,0:T(8,128)S(1)}, u32[]{:S(2)}, u32[]{:S(2)}) collective-permute-start(f32[24,256]{1,0:T(8,128)S(1)} %fusion), channel_id=1, source_target_pairs={{0,48},{4,52},{8,56},{12,60},{16,64},{20,68},{24,72},{28,76},{32,8... | collective-permute-start | bytes 73736
  1358.0 21.9 %collective-permute-start.26 = (f32[24,256]{1,0:T(8,128)S(1)}, f32[24,256]{1,0:T(8,128)S(1)}, u32[]{:S(2)}, u32[]{:S(2)}) collective-permute-start(f32[24,256]{1,0:T(8,128)S(1)} %fusion), channel_id=1, source_target_pairs={{0,44},{4,48},{8,52},{12,56},{16,60},{20,64},{24,68},{28,72},{32,7... | collective-permute-start | bytes 73736
  1359.8 25.0 %collective-permute-start.25 = (f32[24,256]{1,0:T(8,128)S(1)}, f32[24,256]{1,0:T(8,128)S(1)}, u32[]{:S(2)}, u32[]{:S(2)}) collective-permute-start(f32[24,256]{1,0:T(8,128)S(1)} %fusion), channel_id=1, source_target_pairs={{0,40},{4,44},{8,48},{12,52},{16,56},{20,60},{24,64},{28,68},{32,7... | collective-permute-start | bytes 73736
  1372.3 13.8 collective-permute-start.24
  1374.2 20.1 %collective-permute-start.23 = (f32[24,256]{1,0:T(8,128)S(1)}, f32[24,256]{1,0:T(8,128)S(1)}, u32[]{:S(2)}, u32[]{:S(2)}) collective-permute-start(f32[24,256]{1,0:T(8,128)S(1)} %fusion), channel_id=1, source_target_pairs={{0,32},{4,36},{8,40},{12,44},{16,48},{20,52},{24,56},{28,60},{32,6... | collective-permute-start | bytes 73736
  1376.8 21.3 %collective-permute-start.22 = (f32[24,256]{1,0:T(8,128)S(1)}, f32[24,256]{1,0:T(8,128)S(1)}, u32[]{:S(2)}, u32[]{:S(2)}) collective-permute-start(f32[24,256]{1,0:T(8,128)S(1)} %fusion), channel_id=1, source_target_pairs={{0,28},{4,32},{8,36},{12,40},{16,44},{20,48},{24,52},{28,56},{32,6... | collective-permute-start | bytes 73736
  1379.9 22.5 %collective-permute-start.21 = (f32[24,256]{1,0:T(8,128)S(1)}, f32[24,256]{1,0:T(8,128)S(1)}, u32[]{:S(2)}, u32[]{:S(2)}) collective-permute-start(f32[24,256]{1,0:T(8,128)S(1)} %fusion), channel_id=1, source_target_pairs={{0,24},{4,28},{8,32},{12,36},{16,40},{20,44},{24,48},{28,52},{32,5... | collective-permute-start | bytes 73736
  1384.8 21.4 %collective-permute-start.20 = (f32[24,256]{1,0:T(8,128)S(1)}, f32[24,256]{1,0:T(8,128)S(1)}, u32[]{:S(2)}, u32[]{:S(2)}) collective-permute-start(f32[24,256]{1,0:T(8,128)S(1)} %fusion), channel_id=1, source_target_pairs={{0,20},{4,24},{8,28},{12,32},{16,36},{20,40},{24,44},{28,48},{32,5... | collective-permute-start | bytes 73736
  1386.1 20.1 %collective-permute-start.19 = (f32[24,256]{1,0:T(8,128)S(1)}, f32[24,256]{1,0:T(8,128)S(1)}, u32[]{:S(2)}, u32[]{:S(2)}) collective-permute-start(f32[24,256]{1,0:T(8,128)S(1)} %fusion), channel_id=1, source_target_pairs={{0,16},{4,20},{8,24},{12,28},{16,32},{20,36},{24,40},{28,44},{32,4... | collective-permute-start | bytes 73736
  1394.3 11.9 collective-permute-start.18
  1398.1 8.1 collective-permute-start.17
  1402.3 7.8 collective-permute-start.16
  (16 other events, 35.8 us)
Sparse Core Ops, SparseCore 0:
  12.3 202.7 all-gather.10
  219.3 192.8 all-gather.12
  416.8 214.6 all-gather.14
  636.0 213.6 all-gather.8
  960.3 36.5 reduce-scatter.3
where the time goes:
time: 1420 us
  waiting for transfers between devices  826 us (58%)
  blocking collectives  370 us (26%)
  starting transfers between devices  123 us (9%)
  local copies, waits for them, and re-layouts  40 us (3%)
  matrix products  24.2 us (2%)
  other arithmetic  22.4 us (2%)
  between operations  15.5 us (1%)
    unnamed x1, blocking collectives  370 us
    all_gather x1, waiting for transfers between devices, on_device(): lax.all_gather(w_query, 'seq', axis=0, tiled=True)  211 us
    all_gather x1, waiting for transfers between devices, on_device(): lax.all_gather(key_weight, 'seq', axis=0, tiled=True)  204 us
    all_gather x1, waiting for transfers between devices, on_device(): lax.all_gather(value_weight, 'seq', axis=0, tiled=True)  193 us
    all_gather x1, waiting for transfers between devices, on_device(): lax.all_gather(w_out, 'seq', axis=1, tiled=True)  177 us
    unnamed x16, starting transfers between devices  73.4 us
    ppermute x16, starting transfers between devices, passed_along(): return lax.ppermute(array, axis, pairs)  49.4 us
    ppermute x16, waiting for transfers between devices, passed_along(): return lax.ppermute(array, axis, pairs)  34.2 us
  transfers between devices with their start and end apart: 37, of which 8 were waited for; matrix products, arithmetic and copies ran while one was open for 28% of the time, Pallas kernels for 0%

commit v1 on v0

--- a/solution.py
+++ b/solution.py
@@ -8,6 +8,13 @@
 QSCALE = 168
 WINDOW = 1024
 REACH = 8
+
+
+def all_by_exchange(x, mesh_axis, d):
+    devices = lax.axis_size(mesh_axis)
+    blocks = jnp.stack([x for _ in range(devices)])
+    blocks = lax.all_to_all(blocks, mesh_axis, split_axis=0, concat_axis=0)
+    return jnp.concatenate(blocks, axis=d)
 
 
 def passed_along(array, axis, by):
@@ -104,7 +111,7 @@
     key_row_matrix = key_complete.astype(jnp.bfloat16)
     attention_grad = lax.dot_general(
         grad_out,
-        lax.all_gather(w_out, "seq", axis=1, tiled=True),
+        all_by_exchange(w_out, "seq", 1),
         (((1,), (1,)), ((), ())),
         preferred_element_type=jnp.float32,
     ).astype(jnp.bfloat16)

time: 1420 us -> 1230 us (0.87)
  waiting for transfers between devices: 826 us -> 601 us
  starting transfers between devices: 123 us -> 160 us
    all_gather x1 -> x0, waiting for transfers between devices: 177 us -> none  [on_device(): lax.all_gather(w_out, 'seq', axis=1, tiled=True)]
    all_gather x1, waiting for transfers between devices: 211 us -> 176 us  [on_device(): lax.all_gather(w_query, 'seq', axis=0, tiled=True)]
    all_to_all x0 -> x1, starting transfers between devices: none -> 22.2 us  [all_by_exchange(): blocks = lax.all_to_all(blocks, mesh_axis, split_axis=0, concat_axis=0)]
    ppermute x16, waiting for transfers between devices: 34.2 us -> 14.1 us  [passed_along(): return lax.ppermute(array, axis, pairs)]
  transfers between devices with their start and end apart: 37 -> 37, of which waited for: 8 -> 8; matrix products, arithmetic and copies ran while one was open for 28% -> 33% of each run, Pallas kernels for 0% -> 0%
where the time goes in v1:
time: 1230 us
  waiting for transfers between devices  601 us (49%)
  blocking collectives  362 us (29%)
  starting transfers between devices  160 us (13%)
  local copies, waits for them, and re-layouts  45.5 us (4%)
  matrix products  25 us (2%)
  other arithmetic  20.3 us (2%)
  between operations  15.4 us (1%)
    unnamed x1, blocking collectives  362 us
    all_gather x1, waiting for transfers between devices, on_device(): lax.all_gather(key_weight, 'seq', axis=0, tiled=True)  212 us
    all_gather x1, waiting for transfers between devices, on_device(): lax.all_gather(value_weight, 'seq', axis=0, tiled=True)  193 us
    all_gather x1, waiting for transfers between devices, on_device(): lax.all_gather(w_query, 'seq', axis=0, tiled=True)  176 us
    unnamed x16, starting transfers between devices  78.3 us
    ppermute x16, starting transfers between devices, passed_along(): return lax.ppermute(array, axis, pairs)  59.8 us
    unnamed x76, local copies, waits for them, and re-layouts  24.6 us
  transfers between devices with their start and end apart: 37, of which 8 were waited for; matrix products, arithmetic and copies ran while one was open for 33% of the time, Pallas kernels for 0%

profile of v1, /device:TPU:32, one launch (start us, length us, event | category | flops | bytes accessed | tf_op | source)
XLA Modules:
  0.0 1229.7 jit_solution(1825517257365681963)
XLA Ops:
  7.9 2.6 stack.10
  10.5 22.2 %all-to-all-start = ((bf16[128,512,21]{1,2,0:T(8,128)(2,1)}), bf16[128,512,21]{1,2,0:T(8,128)(2,1)}, u32[]{:S(2)}, u32[]{:S(2)}) async-start(bf16[128,512,21]{1,2,0:T(8,128)(2,1)} %stack.10), calls=%async_computation | async-start | bytes 6291456 | tf_op jit(solution)/shard_map/all_to_all | solution.py:16
  34.6 212.4 %all-gather.9.cloned.1.call-done = bf16[128,21,256]{2,1,0:T(8,128)(2,1)} async-done(((bf16[1,21,256]{2,1,0:T(8,128)(2,1)}), bf16[128,21,256]{2,1,0:T(8,128)(2,1)}) %all-gather.9.cloned.1.call-update) | async-done | bytes 1376272 | tf_op jit(solution)/shard_map/all_gather | solution.py:86
  247.0 2.4 reshape.234
  251.3 192.9 %all-gather.11.cloned.1.call-done = bf16[128,21,256]{2,1,0:T(8,128)(2,1)} async-done(((bf16[1,21,256]{2,1,0:T(8,128)(2,1)}), bf16[128,21,256]{2,1,0:T(8,128)(2,1)}) %all-gather.11.cloned.1.call-update) | async-done | bytes 1376272 | tf_op jit(solution)/shard_map/all_gather | solution.py:87
  444.2 2.4 reshape.236
  447.0 4.5 collective-permute-start
  451.5 4.4 collective-permute-start.1
  456.8 4.1 collective-permute-start.2
  460.9 2.8 collective-permute-start.3
  463.8 4.4 collective-permute-start.4
  468.2 3.9 collective-permute-start.5
  472.2 3.3 collective-permute-start.6
  475.6 2.2 collective-permute-start.7
  477.9 3.7 collective-permute-done.6
  481.5 3.1 collective-permute-done.7
  487.6 175.7 %all-gather.7.cloned.1.call-done = bf16[128,21,512]{2,1,0:T(8,128)(2,1)} async-done(((bf16[1,21,512]{2,1,0:T(8,128)(2,1)}), bf16[128,21,512]{2,1,0:T(8,128)(2,1)}) %all-gather.7.cloned.1.call-update) | async-done | bytes 2752528 | tf_op jit(solution)/shard_map/all_gather | solution.py:85
  663.3 3.9 reshape.232
  667.2 2.4 fusion.52
  671.3 1.8 multiply_reduce_fusion.2
  678.3 3.6 fusion.51
  681.9 5.4 reshape.228
  687.3 3.0 convolution_convert_fusion
  691.9 3.6 fusion.10
  695.6 2.5 multiply_reduce_fusion
  708.4 2.4 collective-permute-start.11
  717.0 1.9 multiply_reduce_fusion.1
  722.3 3.5 collective-permute-start.10
  725.8 9.3 collective-permute-start.9
  735.2 9.7 collective-permute-start.8
  744.9 2.1 fusion.33
  747.0 7.3 collective-permute-done.11
  755.9 3.9 fusion.7
  760.4 1.8 copy.113
  772.3 362.0 %fusion = f32[24,256]{1,0:T(8,128)S(1)} fusion(f32[2688,256]{1,0:T(8,128)S(1)} %copy-done.7), kind=kCustom, calls=%all-reduce-scatter | all-reduce-scatter fusion | flops 786433 | bytes 2779136
  1138.3 31.5 %collective-permute-start.28 = (f32[24,256]{1,0:T(8,128)S(1)}, f32[24,256]{1,0:T(8,128)S(1)}, u32[]{:S(2)}, u32[]{:S(2)}) collective-permute-start(f32[24,256]{1,0:T(8,128)S(1)} %fusion), channel_id=1, source_target_pairs={{0,52},{4,56},{8,60},{12,64},{16,68},{20,72},{24,76},{28,80},{32,8... | collective-permute-start | bytes 73736
  1172.4 16.1 %collective-permute-start.25 = (f32[24,256]{1,0:T(8,128)S(1)}, f32[24,256]{1,0:T(8,128)S(1)}, u32[]{:S(2)}, u32[]{:S(2)}) collective-permute-start(f32[24,256]{1,0:T(8,128)S(1)} %fusion), channel_id=1, source_target_pairs={{0,40},{4,44},{8,48},{12,52},{16,56},{20,60},{24,64},{28,68},{32,7... | collective-permute-start | bytes 73736
  1188.5 1.9 collective-permute-start.24
  1190.4 2.5 collective-permute-start.23
  1193.0 3.1 collective-permute-start.22
  1196.0 2.2 collective-permute-start.21
  1198.3 2.5 collective-permute-start.20
  1200.8 4.2 collective-permute-start.19
  1205.1 2.0 collective-permute-start.18
  1207.0 3.9 collective-permute-start.17
  1211.0 1.9 collective-permute-start.16
  1215.1 3.7 collective-permute-done.16
  1218.8 2.1 concatenate.21
  (172 shorter events, 59.6 us)
Async XLA Ops:
  7.2 680.1 %copy-start = (bf16[128,2688]{1,0:T(8,128)(2,1)S(1)}, bf16[128,2688]{1,0:T(8,128)(2,1)}, u32[]{:S(2)}) copy-start(bf16[128,2688]{1,0:T(8,128)(2,1)} %param.10) | copy-start | bytes 2064388
  7.2 239.9 %all-gather.9.cloned.1.call-start = ((), (), s32[]{:S(2)}) async-start(), calls=%async_computation.4 | async-start | bytes 1585152 | tf_op jit(solution)/shard_map/all_gather | solution.py:86
  10.5 23.7 %copy-start.28 = (s32[128]{0:T(128)S(1)}, s32[128]{0:T(128)}, u32[]{:S(2)}) copy-start(s32[128]{0:T(128)} %param.11) | copy-start | bytes 1540
  10.5 671.4 %all-to-all-start = ((bf16[128,512,21]{1,2,0:T(8,128)(2,1)}), bf16[128,512,21]{1,2,0:T(8,128)(2,1)}, u32[]{:S(2)}, u32[]{:S(2)}) async-start(bf16[128,512,21]{1,2,0:T(8,128)(2,1)} %stack.10), calls=%async_computation | async-start | bytes 6291456 | tf_op jit(solution)/shard_map/all_to_all | solution.py:16
  32.7 411.5 %all-gather.11.cloned.1.call-start = ((), (), s32[]{:S(2)}) async-start(), calls=%async_computation.5 | async-start | bytes 1585152 | tf_op jit(solution)/shard_map/all_gather | solution.py:87
  33.4 629.9 %all-gather.7.cloned.1.call-start = ((), (), s32[]{:S(2)}) async-start(), calls=%async_computation.3 | async-start | bytes 3170304 | tf_op jit(solution)/shard_map/all_gather | solution.py:85
  34.2 1187.4 %reduce-scatter.4.cloned.1.call-start = ((), (), s32[]{:S(2)}) async-start(), calls=%async_computation.2 | async-start | bytes 1720320 | tf_op jit(solution)/shard_map/reduce_scatter | solution.py:178
  34.6 216.2 %copy-start.20 = (f32[128,64]{1,0:T(8,128)}, f32[128,64]{1,0:T(8,128)S(1)}, u32[]{:S(2)}) copy-start(f32[128,64]{1,0:T(8,128)S(1)} %get-tuple-element.25) | copy-start | bytes 98308
  34.6 214.8 %copy-start.5 = (bf16[128,2688]{1,0:T(8,128)(2,1)S(1)}, bf16[128,2688]{1,0:T(8,128)(2,1)}, u32[]{:S(2)}) copy-start(bf16[128,2688]{1,0:T(8,128)(2,1)} %param.9) | copy-start | bytes 2064388
  249.9 196.7 %copy-start.13 = (f32[128,2,128]{2,1,0:T(2,128)}, f32[128,2,128]{2,1,0:T(2,128)S(1)}, u32[]{:S(2)}) copy-start(f32[128,2,128]{2,1,0:T(2,128)S(1)} %reshape.226) | copy-start | bytes 393220
  250.6 196.0 %copy-start.23 = (f32[128,2]{1,0:T(8,128)}, f32[128,2]{1,0:T(8,128)S(1)}, u32[]{:S(2)}) copy-start(f32[128,2]{1,0:T(8,128)S(1)} %copy.77) | copy-start | bytes 3076
  446.6 25.5 %copy-start.3 = (bf16[2688,256]{1,0:T(8,128)(2,1)}, bf16[2688,256]{1,0:T(8,128)(2,1)S(1)}, u32[]{:S(2)}) copy-start(bf16[2688,256]{1,0:T(8,128)(2,1)S(1)} %reshape.236) | copy-start | bytes 4128772
  447.0 21.2 %collective-permute-start = (bf16[2,128,256]{2,1,0:T(8,128)(2,1)S(1)}, bf16[2,128,256]{2,1,0:T(8,128)(2,1)S(1)}, u32[]{:S(2)}, u32[]{:S(2)}) collective-permute-start(bf16[2,128,256]{2,1,0:T(8,128)(2,1)S(1)} %pad_maximum_fusion.2), channel_id=1, source_target_pairs={{0,32},{4,36},{8,40},{12,44},{16,48},{20,52},{24,56},{28,60},{32,6... | collective-permute-start | bytes 393224 | tf_op jit(solution)/shard_map/ppermute | solution.py:23
  451.5 20.7 %collective-permute-start.1 = (bf16[2,128,256]{2,1,0:T(8,128)(2,1)S(1)}, bf16[2,128,256]{2,1,0:T(8,128)(2,1)S(1)}, u32[]{:S(2)}, u32[]{:S(2)}) collective-permute-start(bf16[2,128,256]{2,1,0:T(8,128)(2,1)S(1)} %pad_maximum_fusion.2), channel_id=1, source_target_pairs={{0,28},{4,32},{8,36},{12,40},{16,44},{20,48},{24,52},{28,56},{32,6... | collective-permute-start | bytes 393224 | tf_op jit(solution)/shard_map/ppermute | solution.py:23
  456.8 18.7 %collective-permute-start.2 = (bf16[2,128,256]{2,1,0:T(8,128)(2,1)S(1)}, bf16[2,128,256]{2,1,0:T(8,128)(2,1)S(1)}, u32[]{:S(2)}, u32[]{:S(2)}) collective-permute-start(bf16[2,128,256]{2,1,0:T(8,128)(2,1)S(1)} %pad_maximum_fusion.2), channel_id=1, source_target_pairs={{0,24},{4,28},{8,32},{12,36},{16,40},{20,44},{24,48},{28,52},{32,5... | collective-permute-start | bytes 393224 | tf_op jit(solution)/shard_map/ppermute | solution.py:23
  460.9 16.8 %collective-permute-start.3 = (bf16[2,128,256]{2,1,0:T(8,128)(2,1)S(1)}, bf16[2,128,256]{2,1,0:T(8,128)(2,1)S(1)}, u32[]{:S(2)}, u32[]{:S(2)}) collective-permute-start(bf16[2,128,256]{2,1,0:T(8,128)(2,1)S(1)} %pad_maximum_fusion.2), channel_id=1, source_target_pairs={{0,20},{4,24},{8,28},{12,32},{16,36},{20,40},{24,44},{28,48},{32,5... | collective-permute-start | bytes 393224 | tf_op jit(solution)/shard_map/ppermute | solution.py:23
  463.8 14.0 %collective-permute-start.4 = (bf16[2,128,256]{2,1,0:T(8,128)(2,1)S(1)}, bf16[2,128,256]{2,1,0:T(8,128)(2,1)S(1)}, u32[]{:S(2)}, u32[]{:S(2)}) collective-permute-start(bf16[2,128,256]{2,1,0:T(8,128)(2,1)S(1)} %pad_maximum_fusion.2), channel_id=1, source_target_pairs={{0,16},{4,20},{8,24},{12,28},{16,32},{20,36},{24,40},{28,44},{32,4... | collective-permute-start | bytes 393224 | tf_op jit(solution)/shard_map/ppermute | solution.py:23
  468.2 9.6 collective-permute-start.5
  472.2 9.4 collective-permute-start.6
  475.6 9.0 collective-permute-start.7
  703.3 19.1 %collective-permute-start.15 = (f32[2,128,256]{1,2,0:T(8,128)}, f32[2,128,256]{1,2,0:T(8,128)}, u32[]{:S(2)}, u32[]{:S(2)}) collective-permute-start(f32[2,128,256]{1,2,0:T(8,128)} %get-tuple-element.8), channel_id=1, source_target_pairs={{32,0},{36,4},{40,8},{44,12},{48,16},{52,20},{56,24},{60,28},{64,3... | collective-permute-start | bytes 786440 | tf_op jit(solution)/shard_map/ppermute | solution.py:23
  704.5 21.3 %collective-permute-start.14 = (f32[2,128,256]{1,2,0:T(8,128)}, f32[2,128,256]{1,2,0:T(8,128)}, u32[]{:S(2)}, u32[]{:S(2)}) collective-permute-start(f32[2,128,256]{1,2,0:T(8,128)} %get-tuple-element.9), channel_id=1, source_target_pairs={{28,0},{32,4},{36,8},{40,12},{44,16},{48,20},{52,24},{56,28},{60,3... | collective-permute-start | bytes 786440 | tf_op jit(solution)/shard_map/ppermute | solution.py:23
  705.8 29.3 %collective-permute-start.13 = (f32[2,128,256]{1,2,0:T(8,128)}, f32[2,128,256]{1,2,0:T(8,128)}, u32[]{:S(2)}, u32[]{:S(2)}) collective-permute-start(f32[2,128,256]{1,2,0:T(8,128)} %get-tuple-element.7), channel_id=1, source_target_pairs={{24,0},{28,4},{32,8},{36,12},{40,16},{44,20},{48,24},{52,28},{56,3... | collective-permute-start | bytes 786440 | tf_op jit(solution)/shard_map/ppermute | solution.py:23
  707.1 39.9 %collective-permute-start.12 = (f32[2,128,256]{1,2,0:T(8,128)}, f32[2,128,256]{1,2,0:T(8,128)}, u32[]{:S(2)}, u32[]{:S(2)}) collective-permute-start(f32[2,128,256]{1,2,0:T(8,128)} %get-tuple-element.6), channel_id=1, source_target_pairs={{20,0},{24,4},{28,8},{32,12},{36,16},{40,20},{44,24},{48,28},{52,3... | collective-permute-start | bytes 786440 | tf_op jit(solution)/shard_map/ppermute | solution.py:23
  708.4 45.9 %collective-permute-start.11 = (f32[2,128,256]{1,2,0:T(8,128)}, f32[2,128,256]{1,2,0:T(8,128)}, u32[]{:S(2)}, u32[]{:S(2)}) collective-permute-start(f32[2,128,256]{1,2,0:T(8,128)} %get-tuple-element.5), channel_id=1, source_target_pairs={{16,0},{20,4},{24,8},{28,12},{32,16},{36,20},{40,24},{44,28},{48,3... | collective-permute-start | bytes 786440 | tf_op jit(solution)/shard_map/ppermute | solution.py:23
  722.3 32.1 %collective-permute-start.10 = (f32[2,128,256]{1,2,0:T(8,128)}, f32[2,128,256]{1,2,0:T(8,128)S(1)}, u32[]{:S(2)}, u32[]{:S(2)}) collective-permute-start(f32[2,128,256]{1,2,0:T(8,128)} %get-tuple-element.4), channel_id=1, source_target_pairs={{12,0},{16,4},{20,8},{24,12},{28,16},{32,20},{36,24},{40,28},{44,3... | collective-permute-start | bytes 786440 | tf_op jit(solution)/shard_map/ppermute | solution.py:23
  725.8 28.5 %collective-permute-start.9 = (f32[2,128,256]{1,2,0:T(8,128)}, f32[2,128,256]{1,2,0:T(8,128)S(1)}, u32[]{:S(2)}, u32[]{:S(2)}) collective-permute-start(f32[2,128,256]{1,2,0:T(8,128)} %get-tuple-element.3), channel_id=1, source_target_pairs={{8,0},{12,4},{16,8},{20,12},{24,16},{28,20},{32,24},{36,28},{40,32... | collective-permute-start | bytes 786440 | tf_op jit(solution)/shard_map/ppermute | solution.py:23
  735.2 19.2 %collective-permute-start.8 = (f32[2,128,256]{1,2,0:T(8,128)}, f32[2,128,256]{1,2,0:T(8,128)S(1)}, u32[]{:S(2)}, u32[]{:S(2)}) collective-permute-start(f32[2,128,256]{1,2,0:T(8,128)} %get-tuple-element.2), channel_id=1, source_target_pairs={{4,0},{8,4},{12,8},{16,12},{20,16},{24,20},{28,24},{32,28},{36,32}... | collective-permute-start | bytes 786440 | tf_op jit(solution)/shard_map/ppermute | solution.py:23
  744.9 9.5 copy-start.9
  744.9 9.5 copy-start.12
  759.8 8.9 copy-start.2
  759.8 8.9 copy-start.10
  1134.4 36.7 %collective-permute-start.31 = (f32[21,256]{1,0:T(8,128)S(1)}, f32[21,256]{1,0:T(8,128)S(1)}, u32[]{:S(2)}, u32[]{:S(2)}) collective-permute-start(f32[21,256]{1,0:T(8,128)S(1)} %slice.92), channel_id=1, source_target_pairs={{0,64},{4,68},{8,72},{12,76},{16,80},{20,84},{24,88},{28,92},{32,9... | collective-permute-start | bytes 64520
  1135.7 36.7 %collective-permute-start.30 = (f32[24,256]{1,0:T(8,128)S(1)}, f32[24,256]{1,0:T(8,128)S(1)}, u32[]{:S(2)}, u32[]{:S(2)}) collective-permute-start(f32[24,256]{1,0:T(8,128)S(1)} %fusion), channel_id=1, source_target_pairs={{0,60},{4,64},{8,68},{12,72},{16,76},{20,80},{24,84},{28,88},{32,9... | collective-permute-start | bytes 73736
  1137.0 51.5 %collective-permute-start.29 = (f32[24,256]{1,0:T(8,128)S(1)}, f32[24,256]{1,0:T(8,128)S(1)}, u32[]{:S(2)}, u32[]{:S(2)}) collective-permute-start(f32[24,256]{1,0:T(8,128)S(1)} %fusion), channel_id=1, source_target_pairs={{0,56},{4,60},{8,64},{12,68},{16,72},{20,76},{24,80},{28,84},{32,8... | collective-permute-start | bytes 73736
  1138.3 52.2 %collective-permute-start.28 = (f32[24,256]{1,0:T(8,128)S(1)}, f32[24,256]{1,0:T(8,128)S(1)}, u32[]{:S(2)}, u32[]{:S(2)}) collective-permute-start(f32[24,256]{1,0:T(8,128)S(1)} %fusion), channel_id=1, source_target_pairs={{0,52},{4,56},{8,60},{12,64},{16,68},{20,72},{24,76},{28,80},{32,8... | collective-permute-start | bytes 73736
  1169.7 23.2 %collective-permute-start.27 = (f32[24,256]{1,0:T(8,128)S(1)}, f32[24,256]{1,0:T(8,128)S(1)}, u32[]{:S(2)}, u32[]{:S(2)}) collective-permute-start(f32[24,256]{1,0:T(8,128)S(1)} %fusion), channel_id=1, source_target_pairs={{0,48},{4,52},{8,56},{12,60},{16,64},{20,68},{24,72},{28,76},{32,8... | collective-permute-start | bytes 73736
  1171.1 25.0 %collective-permute-start.26 = (f32[24,256]{1,0:T(8,128)S(1)}, f32[24,256]{1,0:T(8,128)S(1)}, u32[]{:S(2)}, u32[]{:S(2)}) collective-permute-start(f32[24,256]{1,0:T(8,128)S(1)} %fusion), channel_id=1, source_target_pairs={{0,44},{4,48},{8,52},{12,56},{16,60},{20,64},{24,68},{28,72},{32,7... | collective-permute-start | bytes 73736
  1172.4 25.9 %collective-permute-start.25 = (f32[24,256]{1,0:T(8,128)S(1)}, f32[24,256]{1,0:T(8,128)S(1)}, u32[]{:S(2)}, u32[]{:S(2)}) collective-permute-start(f32[24,256]{1,0:T(8,128)S(1)} %fusion), channel_id=1, source_target_pairs={{0,40},{4,44},{8,48},{12,52},{16,56},{20,60},{24,64},{28,68},{32,7... | collective-permute-start | bytes 73736
  1188.5 12.3 %collective-permute-start.24 = (f32[24,256]{1,0:T(8,128)S(1)}, f32[24,256]{1,0:T(8,128)S(1)}, u32[]{:S(2)}, u32[]{:S(2)}) collective-permute-start(f32[24,256]{1,0:T(8,128)S(1)} %fusion), channel_id=1, source_target_pairs={{0,36},{4,40},{8,44},{12,48},{16,52},{20,56},{24,60},{28,64},{32,6... | collective-permute-start | bytes 73736
  1190.4 14.6 %collective-permute-start.23 = (f32[24,256]{1,0:T(8,128)S(1)}, f32[24,256]{1,0:T(8,128)S(1)}, u32[]{:S(2)}, u32[]{:S(2)}) collective-permute-start(f32[24,256]{1,0:T(8,128)S(1)} %fusion), channel_id=1, source_target_pairs={{0,32},{4,36},{8,40},{12,44},{16,48},{20,52},{24,56},{28,60},{32,6... | collective-permute-start | bytes 73736
  1193.0 14.1 %collective-permute-start.22 = (f32[24,256]{1,0:T(8,128)S(1)}, f32[24,256]{1,0:T(8,128)S(1)}, u32[]{:S(2)}, u32[]{:S(2)}) collective-permute-start(f32[24,256]{1,0:T(8,128)S(1)} %fusion), channel_id=1, source_target_pairs={{0,28},{4,32},{8,36},{12,40},{16,44},{20,48},{24,52},{28,56},{32,6... | collective-permute-start | bytes 73736
  1196.0 14.9 %collective-permute-start.21 = (f32[24,256]{1,0:T(8,128)S(1)}, f32[24,256]{1,0:T(8,128)S(1)}, u32[]{:S(2)}, u32[]{:S(2)}) collective-permute-start(f32[24,256]{1,0:T(8,128)S(1)} %fusion), channel_id=1, source_target_pairs={{0,24},{4,28},{8,32},{12,36},{16,40},{20,44},{24,48},{28,52},{32,5... | collective-permute-start | bytes 73736
  1198.3 16.6 %collective-permute-start.20 = (f32[24,256]{1,0:T(8,128)S(1)}, f32[24,256]{1,0:T(8,128)S(1)}, u32[]{:S(2)}, u32[]{:S(2)}) collective-permute-start(f32[24,256]{1,0:T(8,128)S(1)} %fusion), channel_id=1, source_target_pairs={{0,20},{4,24},{8,28},{12,32},{16,36},{20,40},{24,44},{28,48},{32,5... | collective-permute-start | bytes 73736
  1200.8 14.0 %collective-permute-start.19 = (f32[24,256]{1,0:T(8,128)S(1)}, f32[24,256]{1,0:T(8,128)S(1)}, u32[]{:S(2)}, u32[]{:S(2)}) collective-permute-start(f32[24,256]{1,0:T(8,128)S(1)} %fusion), channel_id=1, source_target_pairs={{0,16},{4,20},{8,24},{12,28},{16,32},{20,36},{24,40},{28,44},{32,4... | collective-permute-start | bytes 73736
  1205.1 9.8 collective-permute-start.18
  1207.0 8.1 collective-permute-start.17
  1211.0 7.8 collective-permute-start.16
  (18 other events, 40.7 us)
Sparse Core Ops, SparseCore 0:
  12.3 234.7 all-gather.8
  251.3 192.8 all-gather.10
  448.8 214.4 all-gather.6
  771.9 36.5 reduce-scatter.3
